TPU v7x, 256 devices: a whole 4x4x8 slice. The times are simulated.
256 devices in a mesh: gx: 32 (over x, y, core), gy: 8 (over z).
Axes of the slice: x: 4, y: 4, z: 8, core: 2. Of those that a mesh axis runs over, the one named last changes fastest.
Arguments:
- hidden: bfloat16 [1024, 16384], P('gx', 'gy'), may hold values from -40 to 40
- lm_head: bfloat16 [16384, 65536], P('gy', 'gx'), may hold values from -1 to 1
- parent: int32 [1024], replicated, may hold values from 0 to 1023, as said below
- draft_token: int32 [1024], replicated, may hold values from 0 to 65535
- draft_prob: float32 [1024], replicated, may hold values from 0.01 to 1
- uniforms: float32 [1024], replicated, may hold values from 0.01 to 1
- node_count: int32 [16], replicated, may hold values from 1 to 64, as said below
- accepted_end: int32 [16], replicated, may hold values from 0 to 63, as said below
Outputs:
- vertex_accept_slack: float32 [1024], P('gx')
- lineage_least_slack: float32 [1024], P('gx')
- extra_draw_score: float32 [16, 65536], P(None, 'gx')
Inputs may be any that keep to these rules, and one draw needn't show every extreme that they name: A node's parent lies in the same sequence at a lower slot; slot 0 of each sequence is its own parent. `node_count`: some sequence has all 64 slots live. `accepted_end`: the slot of a live node of that sequence.
All inputs are finite; a program needn't handle non-finite values.
Results may differ from a plain program's by a relative error of at most 0.0003.
Values may be sent and summed in bfloat16 or wider, within the bound.
A program may use at most 64 MiB of HBM per device.

v0:
```python
import jax
import jax.numpy as jnp
from jax import lax
from jax.sharding import Mesh
from jax.sharding import PartitionSpec as P

GX = ("gx_0", "gx_1", "gx_2")
big_margin = 10000.0


def in_order(tiles, dim):
    shape = list(tiles.shape[1:])
    shape[dim] *= tiles.shape[0]
    return jnp.moveaxis(tiles, 0, dim).reshape(shape)


def all_blocks(x, axes, sequence):
    tiles = x[None]
    for k in sequence:
        tiles = lax.all_gather(tiles, axes[k], axis=0, tiled=True)
    held = [lax.axis_size(axes[k]) for k in reversed(sequence)]
    tiles = tiles.reshape(*held, *x.shape)
    turned = sorted(range(len(sequence)), key=lambda place: sequence[len(sequence) - 1 - place])
    return tiles.transpose(*turned, *range(len(sequence), tiles.ndim)).reshape(-1, *x.shape)


def whole_of(x, axes, sequence, dim):
    return in_order(all_blocks(x, axes, sequence), dim)


def from_everyone(x, axis):
    copies = jnp.broadcast_to(x, (lax.axis_size(axis), *x.shape))
    return lax.all_to_all(copies, axis, split_axis=0, concat_axis=0, tiled=True)


def all_in_one(x, axis):
    leaves = jax.tree.leaves(x)
    sequence = sorted(range(len(leaves)), key=lambda k: -leaves[k].size)
    width = (1, *leaves[sequence[0]].shape)[-1]
    lines = [
        jnp.pad(leaves[k].reshape(-1), (0, -leaves[k].size % width)).reshape(-1, width)
        for k in sequence
    ]
    both, at, found = (from_everyone(jnp.concatenate(lines), axis), 0, {})
    for k, line in zip(sequence, lines):
        section = both[:, at : at + len(line)].reshape(len(both), -1)
        found[k] = section[:, : leaves[k].size].reshape(-1, *leaves[k].shape)
        at += len(line)
    numbers = iter(range(len(leaves)))
    return jax.tree.map(lambda _: found[next(numbers)], x)


def joined_by_halves(pieces, combine):
    while len(jax.tree.leaves(pieces)[0]) > 1:
        pieces = jax.vmap(combine)(
            *(jax.tree.map(lambda part: part[side::2], pieces) for side in (0, 1))
        )
    return jax.tree.map(lambda part: part[0], pieces)


def combined_all(x, axis, combine):
    pieces = all_in_one(x, axis)
    return joined_by_halves(pieces, combine)


def taken_together(x, axis):
    return from_everyone(x, axis).sum(axis=0)


def together(arrays, axis):
    ends = [0]
    for a in arrays:
        ends.append(ends[-1] + a.size)
    subtotal = taken_together(jnp.concatenate([a.ravel() for a in arrays]), axis)
    return tuple((subtotal[b:e].reshape(a.shape) for a, b, e in zip(arrays, ends, ends[1:])))


def combine_stats(first, second):
    top = jnp.maximum(first[0], second[0])
    total = first[1] * jnp.exp(first[0] - top) + second[1] * jnp.exp(second[0] - top)
    return (top, total, first[2] + second[2])


def local(hidden, lm_head, parent, draft_token, draft_prob, uniforms, node_count, accepted_end):
    out_rows = hidden.shape[0]
    out_start = lax.axis_index(GX) * out_rows
    node_total = parent.shape[0]
    seq_total = node_count.shape[0]
    tree_size = node_total // seq_total
    width = lm_head.shape[1]
    vocab_base = lax.axis_index(GX) * width
    leaf_entries = jnp.arange(seq_total, dtype=jnp.int32) * tree_size + accepted_end
    columns = whole_of(hidden, GX, (1, 0, 2), 0)
    row_count = node_total // lax.axis_size("gy")
    start_row = lax.axis_index("gy") * row_count
    emitted_scores = lax.psum_scatter(
        jnp.dot(columns, lm_head, preferred_element_type=jnp.float32),
        "gy",
        scatter_dimension=0,
        tiled=True,
    )
    own_parent = parent - start_row
    own_token = draft_token - vocab_base
    hit_mask = (own_parent >= 0) & (own_parent < row_count) & (own_token >= 0) & (own_token < width)
    picked = emitted_scores[
        jnp.clip(own_parent, 0, row_count - 1), jnp.clip(own_token, 0, width - 1)
    ]
    target_part = jnp.where(hit_mask, picked, 0.0)
    local_max = jnp.max(emitted_scores, axis=1)
    local_sum = jnp.sum(jnp.exp(emitted_scores - local_max[:, None]), axis=1)
    row_max, row_sum, target_part = combined_all(
        (local_max, local_sum, target_part), GX, combine_stats
    )
    row_log_total = row_max + jnp.log(row_sum)
    total_part = lax.dynamic_update_slice_in_dim(
        jnp.zeros((node_total,), jnp.float32), row_log_total, start_row, 0
    )
    own_end = leaf_entries - start_row
    owned = (own_end >= 0) & (own_end < row_count)
    end_part = jnp.where(owned[:, None], emitted_scores[jnp.clip(own_end, 0, row_count - 1)], 0.0)
    partition_function, target, leaf_scores = together((total_part, target_part, end_part), "gy")
    extra_draw_score = leaf_scores - partition_function[leaf_entries][:, None]
    margin = target - partition_function[parent] - jnp.log(draft_prob) - jnp.log(uniforms)
    node_index = jnp.arange(node_total, dtype=jnp.int32)
    local_index = node_index % tree_size
    live_mask = local_index < node_count[node_index // tree_size]
    root_mask = parent == node_index
    spare_mask = jnp.logical_or(root_mask, jnp.logical_not(live_mask))
    all_margin = jnp.where(spare_mask, 0.0, margin)
    path_min = jnp.where(root_mask, big_margin, margin)
    ancestor = parent
    for _ in range((tree_size - 1).bit_length()):
        path_min = jnp.minimum(path_min, path_min[ancestor])
        ancestor = ancestor[ancestor]
    all_path = jnp.where(spare_mask, 0.0, path_min)
    vertex_accept_slack = lax.dynamic_slice_in_dim(all_margin, out_start, out_rows, 0)
    lineage_least_slack = lax.dynamic_slice_in_dim(all_path, out_start, out_rows, 0)
    return (vertex_accept_slack, lineage_least_slack, extra_draw_score)


def solution(mesh):
    finer = Mesh(mesh.devices.reshape(4, 4, 2, mesh.shape["gy"]), ("gx_0", "gx_1", "gx_2", "gy"))
    placed = (P(GX, "gy"), P("gy", GX), P(), P(), P(), P(), P(), P())
    return jax.shard_map(
        local, mesh=finer, in_specs=placed, out_specs=(P(GX), P(GX), P(None, GX)), check_vma=False
    )
```

profile of v0, /device:TPU:1, one launch (start us, length us, event | category | flops | bytes accessed | tf_op | source)
XLA Modules:
  0.0 307.7 jit_solution(15902408323733157968)
XLA Ops:
  7.2 13.3 %all-gather = bf16[128,2048]{1,0:T(8,128)(2,1)} all-gather(bf16[32,2048]{1,0:T(8,128)(2,1)} %param.8), channel_id=2, replica_groups=mesh['gx_0'=4,'gx_1'=4,'gx_2'=2,'gy'=8] {'gx_1'}, dimensions={0}, use_global_device_ids=true | all-gather | bytes 655360 | tf_op jit(solution)/shard_map/all_gather | solution.py:20
  20.6 37.3 %all-gather.4.cloned.1.call-done = bf16[16,32,2048]{2,1,0:T(8,128)(2,1)} async-done(((bf16[4,32,2048]{2,1,0:T(8,128)(2,1)}), bf16[16,32,2048]{2,1,0:T(8,128)(2,1)}) %all-gather.4.cloned.1.call-update) | async-done | bytes 2097168 | tf_op jit(solution)/shard_map/all_gather | solution.py:20
  57.9 21.7 %all-gather.6.cloned.1.call-done = bf16[32,32,2048]{2,1,0:T(8,128)(2,1)} async-done(((bf16[16,32,2048]{2,1,0:T(8,128)(2,1)}), bf16[32,32,2048]{2,1,0:T(8,128)(2,1)}) %all-gather.6.cloned.1.call-update) | async-done | bytes 4194320 | tf_op jit(solution)/shard_map/all_gather | solution.py:20
  84.3 11.0 %fusion.17 = f32[1024,2048]{1,0:T(8,128)} fusion(bf16[1024,2048]{1,0:T(8,128)(2,1)S(1)} %bitcast.55, bf16[2048,2048]{1,0:T(8,128)(2,1)S(1)} %copy-done.8), kind=kOutput, calls=%fused_computation.94 | convolution fusion | flops 8589934592 | bytes 20971520 | tf_op jit(solution)/shard_map/dot_general | solution.py:97
  96.0 4.5 %gather_fusion.4 = s32[1024]{0:T(1024)S(1)} fusion(s32[1024]{0:T(1024)S(1)} %copy-done, s32[1024]{0:T(1024)S(1)} %get-tuple-element.19), kind=kCustom, calls=%fused_computation.4 | custom fusion | bytes 12288 | tf_op jit(solution)/shard_map/gather | solution.py:134
  100.6 90.3 %reduce-scatter.2.cloned.1.call-done = f32[128,2048]{1,0:T(8,128)} async-done(((f32[1024,2048]{1,0:T(8,128)}), f32[128,2048]{1,0:T(8,128)}) %reduce-scatter.2.cloned.1.call-update) | async-done | bytes 1048592 | tf_op jit(solution)/shard_map/reduce_scatter | solution.py:96
  193.9 8.6 %gather_fusion = f32[1024]{0:T(1024)S(1)} fusion(f32[128,2048]{1,0:T(8,128)S(1)} %copy-done.1, s32[1024]{0:T(1024)S(1)} %get-tuple-element.20), kind=kCustom, calls=%fused_computation | custom fusion | bytes 16384 | tf_op jit(solution)/shard_map/gather | solution.py:105
  203.4 7.6 %all-to-all-start = ((f32[32,3,1024]{2,1,0:T(4,128)}), f32[32,3,1024]{2,1,0:T(4,128)S(1)}, u32[]{:S(2)}, u32[]{:S(2)}) async-start(f32[32,3,1024]{2,1,0:T(4,128)} %broadcast_in_dim.66), calls=%async_computation.1 | async-start | bytes 1048576 | tf_op jit(solution)/shard_map/all_to_all | solution.py:33
  211.0 4.5 %gather_fusion.6 = s32[1024]{0:T(1024)S(1)} fusion(s32[1024]{0:T(1024)S(1)} %gather_fusion.4, s32[1024]{0:T(1024)S(1)} %broadcast_clamp_fusion.4), kind=kCustom, calls=%fused_computation.6 | custom fusion | bytes 12288 | tf_op jit(solution)/shard_map/gather | solution.py:134
  216.3 6.3 %all-to-all-done = f32[32,3,1024]{2,1,0:T(4,128)S(1)} async-done(((f32[32,3,1024]{2,1,0:T(4,128)}), f32[32,3,1024]{2,1,0:T(4,128)S(1)}, u32[]{:S(2)}, u32[]{:S(2)}) %all-to-all-start) | async-done | bytes 393248 | tf_op jit(solution)/shard_map/all_to_all | solution.py:33
  225.4 4.1 %all-to-all-start.1 = ((f32[8,1,34816]{2,1,0:T(1,128)}), f32[8,1,34816]{2,1,0:T(1,128)S(1)}, u32[]{:S(2)}, u32[]{:S(2)}) async-start(f32[8,1,34816]{2,1,0:T(1,128)} %broadcast_in_dim.70), calls=%async_computation.2 | async-start | bytes 2228224 | tf_op jit(solution)/shard_map/all_to_all | solution.py:33
  229.5 4.5 %gather_fusion.8 = s32[1024]{0:T(1024)S(1)} fusion(s32[1024]{0:T(1024)S(1)} %gather_fusion.6, s32[1024]{0:T(1024)S(1)} %broadcast_clamp_fusion.3), kind=kCustom, calls=%fused_computation.8 | custom fusion | bytes 12288 | tf_op jit(solution)/shard_map/gather | solution.py:134
  234.0 4.5 %gather_fusion.10 = s32[1024]{0:T(1024)S(1)} fusion(s32[1024]{0:T(1024)S(1)} %gather_fusion.8, s32[1024]{0:T(1024)S(1)} %broadcast_clamp_fusion.2), kind=kCustom, calls=%fused_computation.10 | custom fusion | bytes 12288 | tf_op jit(solution)/shard_map/gather | solution.py:134
  238.6 4.5 %gather_fusion.12 = s32[1024]{0:T(1024)S(1)} fusion(s32[1024]{0:T(1024)S(1)} %gather_fusion.10, s32[1024]{0:T(1024)S(1)} %broadcast_clamp_fusion.1), kind=kCustom, calls=%fused_computation.12 | custom fusion | bytes 12288 | tf_op jit(solution)/shard_map/gather | solution.py:134
  244.2 4.4 %compare_select_fusion.6 = s32[1024,1]{0,1:T(1,128)S(1)} fusion(s32[]{:T(128)} %bitcast.9, s32[]{:T(128)} %bitcast.10, s32[]{:T(128)} %bitcast.11, s32[]{:T(128)} %bitcast.12, s32[]{:T(128)} %bitcast.13, s32[]{:T(128)} %bitcast.15, s32[]{:T(128)} %bitcast.14), kind=kLoop, calls=%fused_computation.38 | loop fusion | flops 23552 | bytes 4124 | tf_op jit(solution)/shard_map/gather | solution.py:126
  248.6 11.5 %all-to-all-done.1 = f32[8,1,34816]{2,1,0:T(1,128)S(1)} async-done(((f32[8,1,34816]{2,1,0:T(1,128)}), f32[8,1,34816]{2,1,0:T(1,128)S(1)}, u32[]{:S(2)}, u32[]{:S(2)}) %all-to-all-start.1) | async-done | bytes 1114144 | tf_op jit(solution)/shard_map/all_to_all | solution.py:33
  261.0 4.5 %gather_fusion.2 = f32[1024]{0:T(1024)S(1)} fusion(f32[1024]{0:T(1024)S(1)} %slice.224, s32[1024]{0:T(1024)S(1)} %get-tuple-element.19), kind=kCustom, calls=%fused_computation.2 | custom fusion | bytes 12288 | tf_op jit(solution)/shard_map/gather | solution.py:123
  265.5 4.5 %gather_fusion.3 = f32[1024]{0:T(1024)S(1)} fusion(f32[1024]{0:T(1024)S(1)} %get-tuple-element.5, s32[1024]{0:T(1024)S(1)} %get-tuple-element.19), kind=kCustom, calls=%fused_computation.3 | custom fusion | bytes 12288 | tf_op jit(solution)/shard_map/gather | solution.py:133
  270.1 4.5 %gather_fusion.5 = f32[1024]{0:T(1024)S(1)} fusion(f32[1024]{0:T(1024)S(1)} %min.46, s32[1024]{0:T(1024)S(1)} %broadcast_clamp_fusion.4), kind=kCustom, calls=%fused_computation.5 | custom fusion | bytes 12288 | tf_op jit(solution)/shard_map/gather | solution.py:133
  274.7 4.5 %gather_fusion.7 = f32[1024]{0:T(1024)S(1)} fusion(f32[1024]{0:T(1024)S(1)} %min.47, s32[1024]{0:T(1024)S(1)} %broadcast_clamp_fusion.3), kind=kCustom, calls=%fused_computation.7 | custom fusion | bytes 12288 | tf_op jit(solution)/shard_map/gather | solution.py:133
  279.2 4.5 %gather_fusion.9 = f32[1024]{0:T(1024)S(1)} fusion(f32[1024]{0:T(1024)S(1)} %min.48, s32[1024]{0:T(1024)S(1)} %broadcast_clamp_fusion.2), kind=kCustom, calls=%fused_computation.9 | custom fusion | bytes 12288 | tf_op jit(solution)/shard_map/gather | solution.py:133
  283.8 4.5 %gather_fusion.11 = f32[1024]{0:T(1024)S(1)} fusion(f32[1024]{0:T(1024)S(1)} %min.49, s32[1024]{0:T(1024)S(1)} %broadcast_clamp_fusion.1), kind=kCustom, calls=%fused_computation.11 | custom fusion | bytes 12288 | tf_op jit(solution)/shard_map/gather | solution.py:133
  288.3 4.5 %gather_fusion.13 = f32[1024]{0:T(1024)S(1)} fusion(f32[1024]{0:T(1024)S(1)} %min.50, s32[1024]{0:T(1024)S(1)} %broadcast_clamp_fusion), kind=kCustom, calls=%fused_computation.13 | custom fusion | bytes 12288 | tf_op jit(solution)/shard_map/gather | solution.py:133
  292.8 5.7 %minimum_select_fusion = (f32[1024]{0:T(1024)S(1)}, pred[1024]{0:T(1024)(128)(4,1)S(1)}) fusion(f32[1024]{0:T(1024)S(1)} %min.50, f32[1024]{0:T(1024)S(1)} %gather_fusion.13, pred[1024]{0:T(1024)(128)(4,1)S(1)} %get-tuple-element.7, pred[1024]{0:T(1024)(128)(4,1)S(1)} %compare_reduce_fusion, pred[1024]{0:T(1024)(128)(4,1)S(1)} %compare_reduce_fusion.1, ...), kind=kLoop, calls=%fused_computation.66 | loop fusion | flops 20480 | bytes 27684 | tf_op jit(solution)/shard_map/jit(_where)/select_n | solution.py:135
  (118 shorter events, 17.3 us)
Async XLA Ops:
  7.2 50.7 %all-gather.4.cloned.1.call-start = ((), (), s32[]{:S(2)}) async-start(), calls=%async_computation.3 | async-start | bytes 2621440 | tf_op jit(solution)/shard_map/all_gather | solution.py:20
  20.5 59.1 %all-gather.6.cloned.1.call-start = ((), (), s32[]{:S(2)}) async-start(), calls=%async_computation.4 | async-start | bytes 6291456 | tf_op jit(solution)/shard_map/all_gather | solution.py:20
  57.9 133.0 %reduce-scatter.2.cloned.1.call-start = ((), (), s32[]{:S(2)}) async-start(), calls=%async_computation.5 | async-start | bytes 9437184 | tf_op jit(solution)/shard_map/reduce_scatter | solution.py:96
  79.6 4.6 %copy-start.8 = (bf16[2048,2048]{1,0:T(8,128)(2,1)S(1)}, bf16[2048,2048]{1,0:T(8,128)(2,1)}, u32[]{:S(2)}) copy-start(bf16[2048,2048]{1,0:T(8,128)(2,1)} %param.9) | copy-start | bytes 25165828
  95.3 0.7 copy-start
  95.3 0.7 copy-start.4
  95.3 5.2 %copy-start.7 = (s32[16]{0:T(128)S(1)}, s32[16]{0:T(128)}, u32[]{:S(2)}) copy-start(s32[16]{0:T(128)} %param.15) | copy-start | bytes 196
  190.9 3.0 copy-start.1
  203.4 19.2 %all-to-all-start = ((f32[32,3,1024]{2,1,0:T(4,128)}), f32[32,3,1024]{2,1,0:T(4,128)S(1)}, u32[]{:S(2)}, u32[]{:S(2)}) async-start(f32[32,3,1024]{2,1,0:T(4,128)} %broadcast_in_dim.66), calls=%async_computation.1 | async-start | bytes 1048576 | tf_op jit(solution)/shard_map/all_to_all | solution.py:33
  225.4 34.8 %all-to-all-start.1 = ((f32[8,1,34816]{2,1,0:T(1,128)}), f32[8,1,34816]{2,1,0:T(1,128)S(1)}, u32[]{:S(2)}, u32[]{:S(2)}) async-start(f32[8,1,34816]{2,1,0:T(1,128)} %broadcast_in_dim.70), calls=%async_computation.2 | async-start | bytes 2228224 | tf_op jit(solution)/shard_map/all_to_all | solution.py:33
  234.0 9.5 %copy-start.3 = (s32[16]{0:T(128)S(1)}, s32[16]{0:T(128)}, u32[]{:S(2)}) copy-start(s32[16]{0:T(128)} %param.14) | copy-start | bytes 196
  238.6 26.9 %copy-start.5 = (f32[1024]{0:T(1024)S(1)}, f32[1024]{0:T(1024)}, u32[]{:S(2)}) copy-start(f32[1024]{0:T(1024)} %param.13) | copy-start | bytes 12292
  238.6 26.9 %copy-start.6 = (f32[1024]{0:T(1024)S(1)}, f32[1024]{0:T(1024)}, u32[]{:S(2)}) copy-start(f32[1024]{0:T(1024)} %param.12) | copy-start | bytes 12292
  260.9 9.1 %copy-start.2 = (f32[34816]{0:T(1024)}, f32[34816]{0:T(1024)S(1)}, u32[]{:S(2)}) copy-start(f32[34816]{0:T(1024)S(1)} %reduce_sum.19) | copy-start | bytes 417796
  283.7 16.0 %slice-start = ((f32[34816]{0:T(1024)}), f32[32768]{0:T(1024)S(1)}, s32[]{:S(2)}) async-start(f32[34816]{0:T(1024)} %copy-done.2), calls=%async_computation.6 | async-start | bytes 262144 | tf_op jit(solution)/shard_map/slice | solution.py:75
Sparse Core Ops, SparseCore 0:
  20.6 37.1 all-gather.3
  59.7 19.9 all-gather.5
  95.4 95.4 reduce-scatter.1
where the time goes:
time: 308 us
  waiting for transfers between devices  167 us (54%)
  local copies, waits for them, and re-layouts  74.7 us (24%)
  other arithmetic  15.4 us (5%)
  between operations  14.3 us (5%)
  blocking collectives  13.3 us (4%)
  starting transfers between devices  11.8 us (4%)
  matrix products  11 us (4%)
    reduce_scatter x1, waiting for transfers between devices, local(): lax.psum_scatter(jnp.dot(columns, lm_head, preferred_element_type=jnp.flo...  90.3 us
    all_gather x2, waiting for transfers between devices, all_blocks(): tiles = lax.all_gather(tiles, axes[k], axis=0, tiled=True)  59 us
    gather x6, local copies, waits for them, and re-layouts, local(): path_min = jnp.minimum(path_min, path_min[ancestor])  27.2 us
    gather x5, local copies, waits for them, and re-layouts, local(): ancestor = ancestor[ancestor]  22.6 us
    all_to_all x2, waiting for transfers between devices, from_everyone(): return lax.all_to_all(copies, axis, split_axis=0, concat_axis=0, tiled=True)  17.8 us
    all_gather x1, blocking collectives, all_blocks(): tiles = lax.all_gather(tiles, axes[k], axis=0, tiled=True)  13.3 us
    all_to_all x2, starting transfers between devices, from_everyone(): return lax.all_to_all(copies, axis, split_axis=0, concat_axis=0, tiled=True)  11.7 us
    dot_general x1, matrix products, local(): jnp.dot(columns, lm_head, preferred_element_type=jnp.float32)  11 us
  transfers between devices with their start and end apart: 5, of which 5 were waited for; matrix products, arithmetic and copies ran while one was open for 9% of the time, Pallas kernels for 0%

commit v1 on v0

--- a/solution.py
+++ b/solution.py
@@ -17,7 +17,8 @@
 def all_blocks(x, axes, sequence):
     tiles = x[None]
     for k in sequence:
-        tiles = lax.all_gather(tiles, axes[k], axis=0, tiled=True)
+        outgoing = jnp.stack([tiles] * lax.axis_size(axes[k]))
+        tiles = jnp.concatenate(lax.all_to_all(outgoing, axes[k], 0, 0), axis=0)
     held = [lax.axis_size(axes[k]) for k in reversed(sequence)]
     tiles = tiles.reshape(*held, *x.shape)
     turned = sorted(range(len(sequence)), key=lambda place: sequence[len(sequence) - 1 - place])

time: 308 us -> 285 us (0.925)
  waiting for transfers between devices: 167 us -> 106 us
  blocking collectives: 13.3 us -> 51.5 us
    all_gather x2 -> x0, waiting for transfers between devices: 59 us -> none  [all_blocks(): tiles = lax.all_gather(tiles, axes[k], axis=0, tiled=True)]
    all_to_all x0 -> x3, blocking collectives: none -> 51.5 us  [all_blocks(): tiles = jnp.concatenate(lax.all_to_all(outgoing, axes[k], 0, 0), axis=0)]
    all_gather x1 -> x0, blocking collectives: 13.3 us -> none  [all_blocks(): tiles = lax.all_gather(tiles, axes[k], axis=0, tiled=True)]
  transfers between devices with their start and end apart: 5 -> 3, of which waited for: 5 -> 3; matrix products, arithmetic and copies ran while one was open for 9% -> 10% of each run, Pallas kernels for 0% -> 0%
where the time goes in v1:
time: 285 us; the launch traced here: 284 us
  waiting for transfers between devices  106 us (37%)
  local copies, waits for them, and re-layouts  73.5 us (26%)
  blocking collectives  51.5 us (18%)
  other arithmetic  15.8 us (6%)
  between operations  14.7 us (5%)
  starting transfers between devices  11.7 us (4%)
  matrix products  11 us (4%)
    reduce_scatter x1, waiting for transfers between devices, local(): lax.psum_scatter(jnp.dot(columns, lm_head, preferred_element_type=jnp.flo...  88.5 us
    all_to_all x3, blocking collectives, all_blocks(): tiles = jnp.concatenate(lax.all_to_all(outgoing, axes[k], 0, 0), axis=0)  51.5 us
    gather x6, local copies, waits for them, and re-layouts, local(): path_min = jnp.minimum(path_min, path_min[ancestor])  27.2 us
    gather x5, local copies, waits for them, and re-layouts, local(): ancestor = ancestor[ancestor]  22.6 us
    all_to_all x2, waiting for transfers between devices, from_everyone(): return lax.all_to_all(copies, axis, split_axis=0, concat_axis=0, tiled=True)  17.8 us
    all_to_all x2, starting transfers between devices, from_everyone(): return lax.all_to_all(copies, axis, split_axis=0, concat_axis=0, tiled=True)  11.7 us
    dot_general x1, matrix products, local(): jnp.dot(columns, lm_head, preferred_element_type=jnp.float32)  11 us
    gather x1, local copies, waits for them, and re-layouts, local(): emitted_scores[jnp.clip(own_parent, 0, row_count - 1), jnp.clip(own_token...  8.59 us
  transfers between devices with their start and end apart: 3, of which 3 were waited for; matrix products, arithmetic and copies ran while one was open for 10% of the time, Pallas kernels for 0%

profile of v1, /device:TPU:1, one launch (start us, length us, event | category | flops | bytes accessed | tf_op | source)
XLA Modules:
  0.0 284.4 jit_solution(3016915245369915493)
XLA Ops:
  8.2 13.4 %all_to_all.26 = bf16[4,1,32,2048]{3,2,1,0:T(8,128)(2,1)S(1)} all-to-all(bf16[4,1,32,2048]{3,2,1,0:T(8,128)(2,1)S(1)} %stack.9), channel_id=1, replica_groups=mesh['gx_0'=4,'gx_1'=4,'gx_2'=2,'gy'=8] {'gx_1'}, dimensions={0} | all-to-all | bytes 1048576 | tf_op jit(solution)/shard_map/all_to_all | solution.py:21
  21.8 27.9 %all_to_all.27 = bf16[4,4,32,2048]{3,2,1,0:T(8,128)(2,1)S(1)} all-to-all(bf16[4,4,32,2048]{3,2,1,0:T(8,128)(2,1)S(1)} %stack.10), channel_id=1, replica_groups=mesh['gx_0'=4,'gx_1'=4,'gx_2'=2,'gy'=8] {'gx_0'}, dimensions={0} | all-to-all | bytes 4194304 | tf_op jit(solution)/shard_map/all_to_all | solution.py:21
  50.1 10.2 %all_to_all.28 = bf16[2,16,32,2048]{3,2,1,0:T(8,128)(2,1)S(1)} all-to-all(bf16[2,16,32,2048]{3,2,1,0:T(8,128)(2,1)S(1)} %pad_maximum_fusion), channel_id=1, replica_groups=mesh['gx_0'=4,'gx_1'=4,'gx_2'=2,'gy'=8] {'gx_2'}, dimensions={0} | all-to-all | bytes 8388608 | tf_op jit(solution)/shard_map/all_to_all | solution.py:21
  62.5 11.0 %fusion.17 = f32[1024,2048]{1,0:T(8,128)} fusion(bf16[1024,2048]{1,0:T(8,128)(2,1)S(1)} %bitcast.57, bf16[2048,2048]{1,0:T(8,128)(2,1)S(1)} %bitcast.73), kind=kOutput, calls=%fused_computation.95 | convolution fusion | flops 8589934592 | bytes 20971520 | tf_op jit(solution)/shard_map/dot_general | solution.py:98
  74.2 4.5 %gather_fusion.4 = s32[1024]{0:T(1024)S(1)} fusion(s32[1024]{0:T(1024)S(1)} %copy-done, s32[1024]{0:T(1024)S(1)} %get-tuple-element.19), kind=kCustom, calls=%fused_computation.4 | custom fusion | bytes 12288 | tf_op jit(solution)/shard_map/gather | solution.py:135
  78.8 88.5 %reduce-scatter.2.cloned.1.call-done = f32[128,2048]{1,0:T(8,128)} async-done(((f32[1024,2048]{1,0:T(8,128)}), f32[128,2048]{1,0:T(8,128)}) %reduce-scatter.2.cloned.1.call-update) | async-done | bytes 1048592 | tf_op jit(solution)/shard_map/reduce_scatter | solution.py:97
  170.3 8.6 %gather_fusion = f32[1024]{0:T(1024)S(1)} fusion(f32[128,2048]{1,0:T(8,128)S(1)} %copy-done.1, s32[1024]{0:T(1024)S(1)} %get-tuple-element.20), kind=kCustom, calls=%fused_computation | custom fusion | bytes 16384 | tf_op jit(solution)/shard_map/gather | solution.py:106
  179.9 7.6 %all-to-all-start.3 = ((f32[32,3,1024]{2,1,0:T(4,128)}), f32[32,3,1024]{2,1,0:T(4,128)S(1)}, u32[]{:S(2)}, u32[]{:S(2)}) async-start(f32[32,3,1024]{2,1,0:T(4,128)} %broadcast_in_dim.62), calls=%async_computation.4 | async-start | bytes 1048576 | tf_op jit(solution)/shard_map/all_to_all | solution.py:34
  187.5 4.5 %gather_fusion.6 = s32[1024]{0:T(1024)S(1)} fusion(s32[1024]{0:T(1024)S(1)} %gather_fusion.4, s32[1024]{0:T(1024)S(1)} %broadcast_clamp_fusion.4), kind=kCustom, calls=%fused_computation.6 | custom fusion | bytes 12288 | tf_op jit(solution)/shard_map/gather | solution.py:135
  192.7 6.3 %all-to-all-done.3 = f32[32,3,1024]{2,1,0:T(4,128)S(1)} async-done(((f32[32,3,1024]{2,1,0:T(4,128)}), f32[32,3,1024]{2,1,0:T(4,128)S(1)}, u32[]{:S(2)}, u32[]{:S(2)}) %all-to-all-start.3) | async-done | bytes 393248 | tf_op jit(solution)/shard_map/all_to_all | solution.py:34
  201.8 4.1 %all-to-all-start.4 = ((f32[8,1,34816]{2,1,0:T(1,128)}), f32[8,1,34816]{2,1,0:T(1,128)S(1)}, u32[]{:S(2)}, u32[]{:S(2)}) async-start(f32[8,1,34816]{2,1,0:T(1,128)} %broadcast_in_dim.66), calls=%async_computation.5 | async-start | bytes 2228224 | tf_op jit(solution)/shard_map/all_to_all | solution.py:34
  205.9 4.5 %gather_fusion.8 = s32[1024]{0:T(1024)S(1)} fusion(s32[1024]{0:T(1024)S(1)} %gather_fusion.6, s32[1024]{0:T(1024)S(1)} %broadcast_clamp_fusion.3), kind=kCustom, calls=%fused_computation.8 | custom fusion | bytes 12288 | tf_op jit(solution)/shard_map/gather | solution.py:135
  210.5 4.5 %gather_fusion.10 = s32[1024]{0:T(1024)S(1)} fusion(s32[1024]{0:T(1024)S(1)} %gather_fusion.8, s32[1024]{0:T(1024)S(1)} %broadcast_clamp_fusion.2), kind=kCustom, calls=%fused_computation.10 | custom fusion | bytes 12288 | tf_op jit(solution)/shard_map/gather | solution.py:135
  215.1 4.5 %gather_fusion.12 = s32[1024]{0:T(1024)S(1)} fusion(s32[1024]{0:T(1024)S(1)} %gather_fusion.10, s32[1024]{0:T(1024)S(1)} %broadcast_clamp_fusion.1), kind=kCustom, calls=%fused_computation.12 | custom fusion | bytes 12288 | tf_op jit(solution)/shard_map/gather | solution.py:135
  220.6 4.4 %compare_select_fusion.6 = s32[1024,1]{0,1:T(1,128)S(1)} fusion(s32[]{:T(128)} %bitcast.9, s32[]{:T(128)} %bitcast.10, s32[]{:T(128)} %bitcast.11, s32[]{:T(128)} %bitcast.12, s32[]{:T(128)} %bitcast.13, s32[]{:T(128)} %bitcast.15, s32[]{:T(128)} %bitcast.14), kind=kLoop, calls=%fused_computation.39 | loop fusion | flops 23552 | bytes 4124 | tf_op jit(solution)/shard_map/gather | solution.py:127
  225.0 11.5 %all-to-all-done.4 = f32[8,1,34816]{2,1,0:T(1,128)S(1)} async-done(((f32[8,1,34816]{2,1,0:T(1,128)}), f32[8,1,34816]{2,1,0:T(1,128)S(1)}, u32[]{:S(2)}, u32[]{:S(2)}) %all-to-all-start.4) | async-done | bytes 1114144 | tf_op jit(solution)/shard_map/all_to_all | solution.py:34
  237.4 4.5 %gather_fusion.2 = f32[1024]{0:T(1024)S(1)} fusion(f32[1024]{0:T(1024)S(1)} %slice.224, s32[1024]{0:T(1024)S(1)} %get-tuple-element.19), kind=kCustom, calls=%fused_computation.2 | custom fusion | bytes 12288 | tf_op jit(solution)/shard_map/gather | solution.py:124
  242.0 4.5 %gather_fusion.3 = f32[1024]{0:T(1024)S(1)} fusion(f32[1024]{0:T(1024)S(1)} %get-tuple-element.5, s32[1024]{0:T(1024)S(1)} %get-tuple-element.19), kind=kCustom, calls=%fused_computation.3 | custom fusion | bytes 12288 | tf_op jit(solution)/shard_map/gather | solution.py:134
  246.5 4.5 %gather_fusion.5 = f32[1024]{0:T(1024)S(1)} fusion(f32[1024]{0:T(1024)S(1)} %min.46, s32[1024]{0:T(1024)S(1)} %broadcast_clamp_fusion.4), kind=kCustom, calls=%fused_computation.5 | custom fusion | bytes 12288 | tf_op jit(solution)/shard_map/gather | solution.py:134
  251.1 4.5 %gather_fusion.7 = f32[1024]{0:T(1024)S(1)} fusion(f32[1024]{0:T(1024)S(1)} %min.47, s32[1024]{0:T(1024)S(1)} %broadcast_clamp_fusion.3), kind=kCustom, calls=%fused_computation.7 | custom fusion | bytes 12288 | tf_op jit(solution)/shard_map/gather | solution.py:134
  255.6 4.5 %gather_fusion.9 = f32[1024]{0:T(1024)S(1)} fusion(f32[1024]{0:T(1024)S(1)} %min.48, s32[1024]{0:T(1024)S(1)} %broadcast_clamp_fusion.2), kind=kCustom, calls=%fused_computation.9 | custom fusion | bytes 12288 | tf_op jit(solution)/shard_map/gather | solution.py:134
  260.2 4.5 %gather_fusion.11 = f32[1024]{0:T(1024)S(1)} fusion(f32[1024]{0:T(1024)S(1)} %min.49, s32[1024]{0:T(1024)S(1)} %broadcast_clamp_fusion.1), kind=kCustom, calls=%fused_computation.11 | custom fusion | bytes 12288 | tf_op jit(solution)/shard_map/gather | solution.py:134
  264.7 4.5 %gather_fusion.13 = f32[1024]{0:T(1024)S(1)} fusion(f32[1024]{0:T(1024)S(1)} %min.50, s32[1024]{0:T(1024)S(1)} %broadcast_clamp_fusion), kind=kCustom, calls=%fused_computation.13 | custom fusion | bytes 12288 | tf_op jit(solution)/shard_map/gather | solution.py:134
  269.3 5.7 %minimum_select_fusion = (f32[1024]{0:T(1024)S(1)}, pred[1024]{0:T(1024)(128)(4,1)S(1)}) fusion(f32[1024]{0:T(1024)S(1)} %min.50, f32[1024]{0:T(1024)S(1)} %gather_fusion.13, pred[1024]{0:T(1024)(128)(4,1)S(1)} %get-tuple-element.7, pred[1024]{0:T(1024)(128)(4,1)S(1)} %compare_reduce_fusion, pred[1024]{0:T(1024)(128)(4,1)S(1)} %compare_reduce_fusion.1, ...), kind=kLoop, calls=%fused_computation.67 | loop fusion | flops 20480 | bytes 27684 | tf_op jit(solution)/shard_map/jit(_where)/select_n | solution.py:136
  (120 shorter events, 16.3 us)
Async XLA Ops:
  7.2 160.1 %reduce-scatter.2.cloned.1.call-start = ((), (), s32[]{:S(2)}) async-start(), calls=%async_computation.6 | async-start | bytes 9437184 | tf_op jit(solution)/shard_map/reduce_scatter | solution.py:97
  50.1 10.8 %slice-start.1 = ((s8[8388608]{0:T(1024)(128)(4,1)}), s8[4194304]{0:T(1024)(128)(4,1)S(1)}, s32[]{:S(2)}) async-start(s8[8388608]{0:T(1024)(128)(4,1)} %bitcast.72), calls=%async_computation.8 | async-start | bytes 8388608
  60.3 2.2 slice-start.2
  73.5 0.7 copy-start
  73.5 0.7 copy-start.4
  73.5 5.2 %copy-start.7 = (s32[16]{0:T(128)S(1)}, s32[16]{0:T(128)}, u32[]{:S(2)}) copy-start(s32[16]{0:T(128)} %param.15) | copy-start | bytes 196
  167.3 3.0 %copy-start.1 = (f32[128,2048]{1,0:T(8,128)S(1)}, f32[128,2048]{1,0:T(8,128)}, u32[]{:S(2)}) copy-start(f32[128,2048]{1,0:T(8,128)} %reduce-scatter.2.cloned.1.call-done) | copy-start | bytes 3145732
  179.9 19.2 %all-to-all-start.3 = ((f32[32,3,1024]{2,1,0:T(4,128)}), f32[32,3,1024]{2,1,0:T(4,128)S(1)}, u32[]{:S(2)}, u32[]{:S(2)}) async-start(f32[32,3,1024]{2,1,0:T(4,128)} %broadcast_in_dim.62), calls=%async_computation.4 | async-start | bytes 1048576 | tf_op jit(solution)/shard_map/all_to_all | solution.py:34
  201.8 34.8 %all-to-all-start.4 = ((f32[8,1,34816]{2,1,0:T(1,128)}), f32[8,1,34816]{2,1,0:T(1,128)S(1)}, u32[]{:S(2)}, u32[]{:S(2)}) async-start(f32[8,1,34816]{2,1,0:T(1,128)} %broadcast_in_dim.66), calls=%async_computation.5 | async-start | bytes 2228224 | tf_op jit(solution)/shard_map/all_to_all | solution.py:34
  210.5 9.5 %copy-start.3 = (s32[16]{0:T(128)S(1)}, s32[16]{0:T(128)}, u32[]{:S(2)}) copy-start(s32[16]{0:T(128)} %param.14) | copy-start | bytes 196
  215.0 26.9 %copy-start.5 = (f32[1024]{0:T(1024)S(1)}, f32[1024]{0:T(1024)}, u32[]{:S(2)}) copy-start(f32[1024]{0:T(1024)} %param.13) | copy-start | bytes 12292
  215.0 26.9 %copy-start.6 = (f32[1024]{0:T(1024)S(1)}, f32[1024]{0:T(1024)}, u32[]{:S(2)}) copy-start(f32[1024]{0:T(1024)} %param.12) | copy-start | bytes 12292
  237.4 9.1 %copy-start.2 = (f32[34816]{0:T(1024)}, f32[34816]{0:T(1024)S(1)}, u32[]{:S(2)}) copy-start(f32[34816]{0:T(1024)S(1)} %reduce_sum.19) | copy-start | bytes 417796
  260.2 16.0 %slice-start = ((f32[34816]{0:T(1024)}), f32[32768]{0:T(1024)S(1)}, s32[]{:S(2)}) async-start(f32[34816]{0:T(1024)} %copy-done.2), calls=%async_computation.7 | async-start | bytes 262144 | tf_op jit(solution)/shard_map/slice | solution.py:76
Sparse Core Ops, SparseCore 0:
  73.6 93.6 reduce-scatter.1
